TPU v7x, 32 devices: a whole 2x2x4 slice. The times are simulated.
32 devices in a mesh: feat: 8 (over z, y), pair: 4 (over x, core).
Axes of the slice: x: 2, y: 2, z: 4, core: 2. Of those that a mesh axis runs over, the one named last changes fastest.
Arguments:
- in_factors: bfloat16 [512, 2, 512, 256], P(('feat', 'pair')), may hold values from -6 to 6
- out_factors: bfloat16 [512, 2, 512, 256], P(('feat', 'pair')), may hold values from -0.26367188 to 0.26367188
- token_counts: int32 [512, 2], P(('feat', 'pair')), may hold values from 1 to 512, as said below
- slot_pair: int32 [4, 128], P('pair'), may hold values from 0 to 127, each once within a row
- factor_panels: float32 [65536, 1536], P('feat'), as said below
Outputs:
- reduced: float32 [512, 65536], P('pair', 'feat')
Inputs may be any that keep to these rules, and one draw needn't show every extreme that they name: `token_counts`: column 0 counts the chosen response's tokens, column 1 the rejected one's; positions at or beyond the count are padding. `slot_pair`: each row is a permutation of 0 to 127. `factor_panels`: entries above the diagonal in the unknowns' order are zero: rows of panel j hold zeros in the columns of panels after j, and D_k has a positive diagonal.
All inputs are finite; a program needn't handle non-finite values.
Results may differ from a plain program's by a relative error of at most 0.0003.
Values sent between devices are 32-bit elements; how exact they have to be, the bound alone decides.
A program may use at most 128 MiB of HBM per device.

v0:
```python
import jax
import jax.numpy as jnp
from jax import lax
from jax.sharding import PartitionSpec as P

PANEL = 512
PANELS = 3


def spread(value, axis, source):
    kept = jnp.where(lax.axis_index(axis) == source, value, 0).astype(value.dtype)
    return lax.psum(kept, axis)


def panel_product(solved, panel_cols):
    return lax.dot_general(
        solved,
        panel_cols,
        (((1,), (1,)), ((), ())),
        precision=lax.Precision.HIGHEST,
        preferred_element_type=jnp.float32,
    )


def per_device(in_factors, out_factors, token_counts, slot_pair, factor_panels):
    slot_count, side_count, token_depth, proj_rank = in_factors.shape
    n_pair = lax.axis_size("pair")
    n_feat = lax.axis_size("feat")
    per_group = slot_count // n_pair
    row_count = factor_panels.shape[0]
    feat_index = lax.axis_index("feat")
    positions = lax.broadcasted_iota(jnp.int32, (slot_count, side_count, token_depth), 2)
    side_index = lax.broadcasted_iota(jnp.int32, (slot_count, side_count, token_depth), 1)
    weights = jnp.where(
        positions < token_counts[:, :, None], jnp.where(side_index == 0, 1.0, -1.0), 0.0
    ).astype(jnp.bfloat16)
    signed = out_factors * weights[..., None]
    gradients = jnp.einsum("ksti,kstj->kij", signed, in_factors, preferred_element_type=jnp.float32)
    gradients = gradients.reshape(n_pair, per_group, n_feat, row_count)
    group_pairs = slot_pair[0]
    pair_total = n_pair * n_feat * per_group
    outgoing = gradients.transpose(2, 0, 1, 3).reshape(n_feat * n_pair, per_group, row_count)
    received = lax.all_to_all(
        outgoing, ("feat", "pair"), split_axis=0, concat_axis=1, tiled=True
    ).reshape(pair_total, row_count)
    pair_rows = lax.broadcasted_iota(jnp.int32, (pair_total, pair_total), 0)
    placement = (pair_rows == group_pairs[None, :]).astype(jnp.float32)
    right_side = jnp.dot(
        placement, received, precision=lax.Precision.HIGHEST, preferred_element_type=jnp.float32
    )
    identity = jnp.eye(PANEL, dtype=jnp.float32)

    def solve_panel(k, current):
        diagonal = jnp.where(
            feat_index == k, factor_panels[:PANEL, k * PANEL : (k + 1) * PANEL], identity
        )
        solved = jax.scipy.linalg.solve_triangular(diagonal, current[:, :PANEL].T, lower=True).T
        return spread(solved, "feat", k)

    solved = solve_panel(0, right_side)
    for k in range(PANELS):
        panel_cols = factor_panels[:, k * PANEL : (k + 1) * PANEL]
        head_rows = right_side[:, :PANEL] - panel_product(solved, panel_cols[:PANEL])
        head_rows = jnp.where(feat_index == k, solved, head_rows)
        following = solved
        if k + 1 < PANELS:
            following = solve_panel(k + 1, head_rows)
        tail_rows = right_side[:, PANEL:] - panel_product(solved, panel_cols[PANEL:])
        right_side = jnp.concatenate([head_rows, tail_rows], axis=1)
        solved = following
    return right_side


def solution(mesh):
    return jax.shard_map(
        per_device,
        mesh=mesh,
        in_specs=(
            P(("feat", "pair"), None, None, None),
            P(("feat", "pair"), None, None, None),
            P(("feat", "pair"), None),
            P("pair", None),
            P("feat", None),
        ),
        out_specs=P("pair", "feat"),
        check_vma=False,
    )
```

profile of v0, /device:TPU:0, one launch (start us, length us, event | category | flops | bytes accessed | tf_op | source)
XLA Modules:
  0.0 420.1 jit_solution(17209154780739720358)
XLA Ops:
  6.5 0.8 copy.20
  7.4 9.8 %fusion.18 = f32[16,256,256]{2,1,0:T(8,128)} fusion(bf16[16,2,512,256]{3,2,1,0:T(8,128)(2,1)} %param.7, bf16[16,2,512,256]{3,2,1,0:T(8,128)(2,1)} %param.8, bf16[16,2,512]{2,1,0:T(2,128)(2,1)S(1)} %fusion.63), kind=kOutput, calls=%fused_computation.19 | convolution fusion | flops 2151677952 | bytes 21004288 | tf_op jit(solution)/shard_map/ksti,kstj->kij/dot_general | solution.py:38
  17.3 5.0 %reshape.28 = f32[4,4,8,8192]{3,2,1,0:T(8,128)} reshape(f32[16,256,256]{2,1,0:T(8,128)} %fusion.18) | data formatting | bytes 8388608 | tf_op jit(solution)/shard_map/reshape | solution.py:39
  22.2 6.9 %copy.22 = f32[4,4,8,8192]{3,1,0,2:T(4,128)} copy(f32[4,4,8,8192]{3,2,1,0:T(8,128)} %reshape.28) | data formatting | bytes 8388608 | tf_op jit(solution)/shard_map/reshape | solution.py:39
  29.1 7.5 %all-to-all-start = ((f32[32,4,8192]{2,1,0:T(4,128)}), f32[32,4,8192]{2,1,0:T(4,128)}, u32[]{:S(2)}, u32[]{:S(2)}) async-start(f32[32,4,8192]{2,1,0:T(4,128)} %bitcast.103), calls=%async_computation | async-start | bytes 8388608 | tf_op jit(solution)/shard_map/all_to_all | solution.py:43
  37.0 2.3 fusion.24
  39.3 8.4 %while.6 = (s32[]{:T(128)}, f32[512,512]{1,0:T(8,128)S(1)}, s32[4,2]{0,1:T(2,128)S(1)}, f32[4,128,128]{2,1,0:T(8,128)S(1)}, s32[]{:T(128)}) while((s32[]{:T(128)}, f32[512,512]{1,0:T(8,128)S(1)}, s32[4,2]{0,1:T(2,128)S(1)}, f32[4,128,128]{2,1,0:T(8,128)S(1)}, s32[]{:T(128)}) %tuple.51), condition=%wide.while_cond, body=%wide.while_body.sunk | while | flops 2 | bytes 131189 | solution.py:57
  39.4 0.6 fusion.116
  40.0 1.4 bitcast_dynamic-update-slice_fusion.6
  41.5 0.6 fusion.116
  42.1 1.4 bitcast_dynamic-update-slice_fusion.6
  43.6 0.6 fusion.116
  44.2 1.4 bitcast_dynamic-update-slice_fusion.6
  46.3 1.4 bitcast_dynamic-update-slice_fusion.6
  47.7 0.7 copy-done.4
  48.4 40.1 %custom-call.5 = f32[4,128,128]{1,2,0:T(8,128)S(1)} custom-call(f32[4,128,128]{2,1,0:T(8,128)} %copy-done.4), custom_call_target="InvertDiagBlocksLowerTriangular" | custom-call | tf_op jit(solution)/shard_map/jit(_solve_triangular)/triangular_solve | solution.py:57
  88.6 0.8 broadcast.62.clone.1
  89.3 9.7 %while.7 = (s32[]{:T(128)}, f32[512,512]{1,0:T(8,128)S(1)}, s32[4,2]{0,1:T(2,128)S(1)}, f32[4,128,128]{2,1,0:T(8,128)}, s32[]{:T(128)}) while((s32[]{:T(128)}, f32[512,512]{1,0:T(8,128)S(1)}, s32[4,2]{0,1:T(2,128)S(1)}, f32[4,128,128]{2,1,0:T(8,128)}, s32[]{:T(128)}) %tuple.66), condition=%wide.while_cond.clone, body=%wide.while_body.clone.sunk | while | flops 2 | bytes 132205 | solution.py:57
  89.9 1.8 bitcast_dynamic-update-slice_fusion.7
  92.3 1.8 bitcast_dynamic-update-slice_fusion.7
  94.8 1.8 bitcast_dynamic-update-slice_fusion.7
  97.2 1.8 bitcast_dynamic-update-slice_fusion.7
  99.0 31.2 %all-to-all-done = f32[32,4,8192]{2,1,0:T(4,128)} async-done(((f32[32,4,8192]{2,1,0:T(4,128)}), f32[32,4,8192]{2,1,0:T(4,128)}, u32[]{:S(2)}, u32[]{:S(2)}) %all-to-all-start) | async-done | bytes 4194336 | tf_op jit(solution)/shard_map/all_to_all | solution.py:43
  130.3 5.3 %reshape.30 = f32[128,8192]{1,0:T(8,128)} reshape(f32[32,4,8192]{2,1,0:T(4,128)} %all-to-all-done) | data formatting | bytes 8388608 | tf_op jit(solution)/shard_map/reshape | solution.py:45
  135.5 4.5 %fusion.82 = f32[128,8192]{1,0:T(8,128)S(1)} fusion(f32[128,8192]{1,0:T(8,128)} %reshape.30, s32[128]{0:T(128)S(1)} %bitcast.112), kind=kOutput, calls=%fused_computation.116 | convolution fusion | flops 1610629120 | bytes 8389120 | tf_op jit(solution)/shard_map/dot_general | solution.py:48
  140.1 2.0 copy-done
  143.4 1.1 fusion.77
  145.3 1.1 fusion.76
  146.4 0.7 fusion.30
  147.2 0.6 all-reduce.6.cloned.1.call-start
  147.8 7.8 %while.8 = (s32[]{:T(128)}, f32[512,512]{1,0:T(8,128)S(1)}, s32[4,2]{0,1:T(2,128)S(1)}, f32[4,128,128]{2,1,0:T(8,128)S(1)}, s32[]{:T(128)}) while((s32[]{:T(128)}, f32[512,512]{1,0:T(8,128)S(1)}, s32[4,2]{0,1:T(2,128)S(1)}, f32[4,128,128]{2,1,0:T(8,128)S(1)}, s32[]{:T(128)}) %tuple.67), condition=%wide.while_cond.clone.1, body=%wide.while_body.clone.1.sunk | while | flops 2 | bytes 131189 | solution.py:57
  148.5 1.3 bitcast_dynamic-update-slice_fusion.8
  150.4 1.3 bitcast_dynamic-update-slice_fusion.8
  152.4 1.3 bitcast_dynamic-update-slice_fusion.8
  154.3 1.3 bitcast_dynamic-update-slice_fusion.8
  155.6 40.1 %custom-call.6 = f32[4,128,128]{1,2,0:T(8,128)S(1)} custom-call(f32[4,128,128]{2,1,0:T(8,128)} %get-tuple-element.27), custom_call_target="InvertDiagBlocksLowerTriangular" | custom-call | tf_op jit(solution)/shard_map/jit(_solve_triangular)/triangular_solve | solution.py:57
  195.8 39.3 %custom-call.7 = f32[4,128,128]{1,2,0:T(8,128)S(1)} custom-call(f32[4,128,128]{2,1,0:T(8,128)S(1)} %get-tuple-element.28), custom_call_target="InvertDiagBlocksLowerTriangular" | custom-call | tf_op jit(solution)/shard_map/jit(_solve_triangular)/triangular_solve | solution.py:57
  235.1 2.6 fusion.23
  240.3 0.7 fusion.31
  241.3 21.2 %fusion.6 = f32[128,7680]{1,0:T(8,128)} fusion(f32[128,512]{1,0:T(8,128)S(1)} %copy-done.1, f32[8192,1536]{1,0:T(8,128)} %param.11, f32[128,8192]{1,0:T(8,128)} %copy-done), kind=kOutput, calls=%fused_computation.12 | convolution fusion | flops 6040780800 | bytes 23855104 | tf_op jit(solution)/shard_map/dot_general | solution.py:16
  262.5 49.2 %all-reduce.6.cloned.1.call-done = f32[128,512]{1,0:T(8,128)} async-done(((f32[128,512]{1,0:T(8,128)}), f32[128,512]{1,0:T(8,128)}) %all-reduce.6.cloned.1.call-update) | async-done | bytes 262160 | tf_op jit(solution)/shard_map/psum | solution.py:12
  311.7 2.6 fusion.22
  316.9 0.7 fusion.32
  317.6 23.0 %fusion.9 = f32[128,7680]{1,0:T(8,128)} fusion(f32[128,7680]{1,0:T(8,128)} %fusion.6, f32[128,512]{1,0:T(8,128)S(1)} %copy-done.2, f32[8192,1536]{1,0:T(8,128)} %param.11), kind=kOutput, calls=%fused_computation.13 | convolution fusion | flops 6040780800 | bytes 23855104 | tf_op jit(solution)/shard_map/dot_general | solution.py:16
  340.6 47.4 %all-reduce.8.cloned.1.call-done = f32[128,512]{1,0:T(8,128)} async-done(((f32[128,512]{1,0:T(8,128)}), f32[128,512]{1,0:T(8,128)}) %all-reduce.8.cloned.1.call-update) | async-done | bytes 262160 | tf_op jit(solution)/shard_map/psum | solution.py:12
  388.0 2.5 fusion.21
  390.5 20.4 %fusion.12 = f32[128,7680]{1,0:T(8,128)S(1)} fusion(f32[128,7680]{1,0:T(8,128)} %fusion.9, f32[128,512]{1,0:T(8,128)} %all-reduce.8.cloned.1.call-done, f32[8192,1536]{1,0:T(8,128)} %param.11), kind=kOutput, calls=%fused_computation.14 | convolution fusion | flops 6040780800 | bytes 23855104 | tf_op jit(solution)/shard_map/dot_general | solution.py:16
  411.0 2.3 pad_maximum_fusion
  (72 shorter events, 13.8 us)
Async XLA Ops:
  29.1 101.2 %all-to-all-start = ((f32[32,4,8192]{2,1,0:T(4,128)}), f32[32,4,8192]{2,1,0:T(4,128)}, u32[]{:S(2)}, u32[]{:S(2)}) async-start(f32[32,4,8192]{2,1,0:T(4,128)} %bitcast.103), calls=%async_computation | async-start | bytes 8388608 | tf_op jit(solution)/shard_map/all_to_all | solution.py:43
  36.6 198.5 %all-reduce.4.cloned.1.call-start = ((), (), s32[]{:S(2)}) async-start(), calls=%async_computation.1 | async-start | bytes 524288 | tf_op jit(solution)/shard_map/psum | solution.py:12
  47.7 0.7 copy-start.4
  88.6 54.2 %copy-start.3 = (f32[4,128,128]{1,2,0:T(8,128)}, f32[4,128,128]{1,2,0:T(8,128)S(1)}, u32[]{:S(2)}) copy-start(f32[4,128,128]{1,2,0:T(8,128)S(1)} %custom-call.5) | copy-start | bytes 786436
  99.0 36.5 %copy-start.5 = (s32[1,128]{1,0:T(1,128)S(1)}, s32[1,128]{1,0:T(1,128)}, u32[]{:S(2)}) copy-start(s32[1,128]{1,0:T(1,128)} %param.10) | copy-start | bytes 1540
  140.1 2.0 copy-start
  147.2 164.6 %all-reduce.6.cloned.1.call-start = ((), (), s32[]{:S(2)}) async-start(), calls=%async_computation.2 | async-start | bytes 524288 | tf_op jit(solution)/shard_map/psum | solution.py:12
  235.1 6.2 %copy-start.1 = (f32[128,512]{1,0:T(8,128)S(1)}, f32[128,512]{1,0:T(8,128)}, u32[]{:S(2)}) copy-start(f32[128,512]{1,0:T(8,128)} %all-reduce.4.cloned.1.call-done) | copy-start | bytes 786436
  241.1 146.9 %all-reduce.8.cloned.1.call-start = ((), (), s32[]{:S(2)}) async-start(), calls=%async_computation.3 | async-start | bytes 524288 | tf_op jit(solution)/shard_map/psum | solution.py:12
  311.7 5.9 %copy-start.2 = (f32[128,512]{1,0:T(8,128)S(1)}, f32[128,512]{1,0:T(8,128)}, u32[]{:S(2)}) copy-start(f32[128,512]{1,0:T(8,128)} %all-reduce.6.cloned.1.call-done) | copy-start | bytes 786436
Sparse Core Ops, SparseCore 0:
  147.3 71.4 all-reduce.3
  241.2 70.4 all-reduce.5
  317.8 70.1 all-reduce.7
where the time goes:
time: 425 us; the launch traced here: 420 us
  waiting for transfers between devices  128 us (30%)
  other arithmetic  126 us (30%)
  matrix products  95.1 us (22%)
  local copies, waits for them, and re-layouts  48 us (11%)
  between operations  13.8 us (3%)
  starting transfers between devices  8.67 us (2%)
    another operation x5, other arithmetic, solve_panel(): jax.scipy.linalg.solve_triangular(diagonal, current[:, :PANEL].T, lower=T...  122 us
    psum x3, waiting for transfers between devices, spread(): return lax.psum(kept, axis)  96.6 us
    dot_general x6, matrix products, panel_product(): lax.dot_general(solved, panel_cols, (((1,), (1,)), ((), ())), precision=l...  72.3 us
    all_to_all x1, waiting for transfers between devices, per_device(): lax.all_to_all(outgoing, ('feat', 'pair'), split_axis=0, concat_axis=1, t...  31.2 us
    another operation x49, local copies, waits for them, and re-layouts, solve_panel(): jax.scipy.linalg.solve_triangular(diagonal, current[:, :PANEL].T, lower=T...  27.4 us
    reshape x2, local copies, waits for them, and re-layouts, per_device(): gradients = gradients.reshape(n_pair, per_group, n_feat, row_count)  11.9 us
    dot_general x1, matrix products, per_device(): jnp.einsum('ksti,kstj->kij', signed, in_factors, preferred_element_type=j...  9.84 us
  transfers between devices with their start and end apart: 4, of which 3 were waited for; matrix products, arithmetic and copies ran while one was open for 46% of the time, Pallas kernels for 0%

commit v1 on v0

--- a/solution.py
+++ b/solution.py
@@ -40,8 +40,14 @@
     group_pairs = slot_pair[0]
     pair_total = n_pair * n_feat * per_group
     outgoing = gradients.transpose(2, 0, 1, 3).reshape(n_feat * n_pair, per_group, row_count)
-    received = lax.all_to_all(
-        outgoing, ("feat", "pair"), split_axis=0, concat_axis=1, tiled=True
+    received = jnp.concatenate(
+        lax.all_to_all(
+            jnp.stack(jnp.split(outgoing, lax.axis_size(("feat", "pair")), axis=0)),
+            ("feat", "pair"),
+            0,
+            0,
+        ),
+        axis=1,
     ).reshape(pair_total, row_count)
     pair_rows = lax.broadcasted_iota(jnp.int32, (pair_total, pair_total), 0)
     placement = (pair_rows == group_pairs[None, :]).astype(jnp.float32)

time: 425 us -> 445 us (1.047)
  local copies, waits for them, and re-layouts: 48 us -> 67.2 us
    unnamed x13 -> x44, local copies, waits for them, and re-layouts: 3.47 us -> 24 us
    another operation x0 -> x2, local copies, waits for them, and re-layouts: none -> 5.94 us  [the longest x1 5.27 us: per_device(): received = jnp.concatenate(lax.all_to_all(jnp.stack(jnp.split(outgoing, l...]
    reshape x1 -> x0, local copies, waits for them, and re-layouts: 5.27 us -> none  [per_device(): received = lax.all_to_all(outgoing, ('feat', 'pair'), split_axis=0, conca...]
  transfers between devices with their start and end apart: 4 -> 4, of which waited for: 3 -> 3; matrix products, arithmetic and copies ran while one was open for 46% -> 44% of each run, Pallas kernels for 0% -> 0%
where the time goes in v1:
time: 445 us; the launch traced here: 439 us
  waiting for transfers between devices  128 us (29%)
  other arithmetic  126 us (28%)
  matrix products  95 us (21%)
  local copies, waits for them, and re-layouts  67.2 us (15%)
  between operations  13.8 us (3%)
  starting transfers between devices  8.67 us (2%)
    another operation x5, other arithmetic, solve_panel(): jax.scipy.linalg.solve_triangular(diagonal, current[:, :PANEL].T, lower=T...  122 us
    psum x3, waiting for transfers between devices, spread(): return lax.psum(kept, axis)  96.7 us
    dot_general x6, matrix products, panel_product(): lax.dot_general(solved, panel_cols, (((1,), (1,)), ((), ())), precision=l...  72.3 us
    all_to_all x1, waiting for transfers between devices, per_device(): lax.all_to_all(jnp.stack(jnp.split(outgoing, lax.axis_size(('feat', 'pair...  31.2 us
    another operation x49, local copies, waits for them, and re-layouts, solve_panel(): jax.scipy.linalg.solve_triangular(diagonal, current[:, :PANEL].T, lower=T...  27.4 us
    unnamed x44, local copies, waits for them, and re-layouts  24 us
    dot_general x1, matrix products, per_device(): jnp.einsum('ksti,kstj->kij', signed, in_factors, preferred_element_type=j...  9.84 us
    reshape x2, local copies, waits for them, and re-layouts, per_device(): gradients = gradients.reshape(n_pair, per_group, n_feat, row_count)  9.84 us
  transfers between devices with their start and end apart: 4, of which 3 were waited for; matrix products, arithmetic and copies ran while one was open for 44% of the time, Pallas kernels for 0%

profile of v1, /device:TPU:0, one launch (start us, length us, event | category | flops | bytes accessed | tf_op | source)
XLA Modules:
  0.0 439.3 jit_solution(14972404944218895282)
XLA Ops:
  6.5 0.8 copy.20
  7.4 9.8 %fusion.18 = f32[16,256,256]{2,1,0:T(8,128)} fusion(bf16[16,2,512,256]{3,2,1,0:T(8,128)(2,1)} %param.7, bf16[16,2,512,256]{3,2,1,0:T(8,128)(2,1)} %param.8, bf16[16,2,512]{2,1,0:T(2,128)(2,1)S(1)} %fusion.95), kind=kOutput, calls=%fused_computation.19 | convolution fusion | flops 2151677952 | bytes 21004288 | tf_op jit(solution)/shard_map/ksti,kstj->kij/dot_general | solution.py:38
  17.3 5.0 %reshape.21 = f32[4,4,8,8192]{3,2,1,0:T(8,128)} reshape(f32[16,256,256]{2,1,0:T(8,128)} %fusion.18) | data formatting | bytes 8388608 | tf_op jit(solution)/shard_map/reshape | solution.py:39
  22.2 4.9 %copy.22 = f32[4,4,8,8192]{3,1,0,2:T(4,128)S(1)} copy(f32[4,4,8,8192]{3,2,1,0:T(8,128)} %reshape.21) | data formatting | bytes 8388608 | tf_op jit(solution)/shard_map/reshape | solution.py:39
  27.1 0.7 fusion.85
  29.1 0.7 fusion.82
  30.4 0.7 fusion.80
  31.7 0.7 fusion.78
  48.4 7.5 %all-to-all-start = ((f32[32,1,4,8192]{3,2,1,0:T(4,128)}), f32[32,1,4,8192]{3,2,1,0:T(4,128)}, u32[]{:S(2)}, u32[]{:S(2)}) async-start(f32[32,1,4,8192]{3,2,1,0:T(4,128)} %fusion.54), calls=%async_computation | async-start | bytes 8388608 | tf_op jit(solution)/shard_map/all_to_all | solution.py:44
  56.2 2.3 fusion.24
  58.5 8.4 %while.6 = (s32[]{:T(128)}, f32[512,512]{1,0:T(8,128)S(1)}, s32[4,2]{0,1:T(2,128)S(1)}, f32[4,128,128]{2,1,0:T(8,128)S(1)}, s32[]{:T(128)}) while((s32[]{:T(128)}, f32[512,512]{1,0:T(8,128)S(1)}, s32[4,2]{0,1:T(2,128)S(1)}, f32[4,128,128]{2,1,0:T(8,128)S(1)}, s32[]{:T(128)}) %tuple.51), condition=%wide.while_cond, body=%wide.while_body.sunk | while | flops 2 | bytes 131181 | solution.py:63
  59.2 1.4 bitcast_dynamic-update-slice_fusion.6
  61.3 1.4 bitcast_dynamic-update-slice_fusion.6
  63.4 1.4 bitcast_dynamic-update-slice_fusion.6
  65.6 1.4 bitcast_dynamic-update-slice_fusion.6
  67.0 0.7 copy-done.4
  67.7 40.1 %custom-call.5 = f32[4,128,128]{1,2,0:T(8,128)S(1)} custom-call(f32[4,128,128]{2,1,0:T(8,128)} %copy-done.4), custom_call_target="InvertDiagBlocksLowerTriangular" | custom-call | tf_op jit(solution)/shard_map/jit(_solve_triangular)/triangular_solve | solution.py:63
  107.8 0.8 broadcast.62.clone.1
  108.6 9.7 %while.7 = (s32[]{:T(128)}, f32[512,512]{1,0:T(8,128)S(1)}, s32[4,2]{0,1:T(2,128)S(1)}, f32[4,128,128]{2,1,0:T(8,128)}, s32[]{:T(128)}) while((s32[]{:T(128)}, f32[512,512]{1,0:T(8,128)S(1)}, s32[4,2]{0,1:T(2,128)S(1)}, f32[4,128,128]{2,1,0:T(8,128)}, s32[]{:T(128)}) %tuple.66), condition=%wide.while_cond.clone, body=%wide.while_body.clone.sunk | while | flops 2 | bytes 132705 | solution.py:63
  109.2 1.8 bitcast_dynamic-update-slice_fusion.7
  111.6 1.8 bitcast_dynamic-update-slice_fusion.7
  114.0 1.8 bitcast_dynamic-update-slice_fusion.7
  116.4 1.8 bitcast_dynamic-update-slice_fusion.7
  118.3 31.2 %all-to-all-done = f32[32,1,4,8192]{3,2,1,0:T(4,128)} async-done(((f32[32,1,4,8192]{3,2,1,0:T(4,128)}), f32[32,1,4,8192]{3,2,1,0:T(4,128)}, u32[]{:S(2)}, u32[]{:S(2)}) %all-to-all-start) | async-done | bytes 4194336 | tf_op jit(solution)/shard_map/all_to_all | solution.py:44
  149.5 5.3 %reshape_reshape.3 = f32[128,8192]{1,0:T(8,128)} reshape(f32[32,1,4,8192]{3,2,1,0:T(4,128)} %all-to-all-done) | data formatting | bytes 8388608 | tf_op jit(solution)/shard_map/reshape;reshape | solution.py:51
  154.8 4.5 %fusion.114 = f32[128,8192]{1,0:T(8,128)S(1)} fusion(f32[128,8192]{1,0:T(8,128)} %reshape_reshape.3, s32[128]{0:T(128)S(1)} %bitcast.271), kind=kOutput, calls=%fused_computation.180 | convolution fusion | flops 1610629120 | bytes 8389120 | tf_op jit(solution)/shard_map/dot_general | solution.py:54
  159.3 2.0 copy-done
  162.7 1.1 fusion.109
  164.6 1.1 fusion.108
  165.6 0.7 fusion.30
  167.1 7.8 %while.8 = (s32[]{:T(128)}, f32[512,512]{1,0:T(8,128)S(1)}, s32[4,2]{0,1:T(2,128)S(1)}, f32[4,128,128]{2,1,0:T(8,128)S(1)}, s32[]{:T(128)}) while((s32[]{:T(128)}, f32[512,512]{1,0:T(8,128)S(1)}, s32[4,2]{0,1:T(2,128)S(1)}, f32[4,128,128]{2,1,0:T(8,128)S(1)}, s32[]{:T(128)}) %tuple.67), condition=%wide.while_cond.clone.1, body=%wide.while_body.clone.1.sunk | while | flops 2 | bytes 131181 | solution.py:63
  167.7 1.3 bitcast_dynamic-update-slice_fusion.8
  169.7 1.3 bitcast_dynamic-update-slice_fusion.8
  171.6 1.3 bitcast_dynamic-update-slice_fusion.8
  173.6 1.3 bitcast_dynamic-update-slice_fusion.8
  174.9 40.1 %custom-call.6 = f32[4,128,128]{1,2,0:T(8,128)S(1)} custom-call(f32[4,128,128]{2,1,0:T(8,128)} %get-tuple-element.27), custom_call_target="InvertDiagBlocksLowerTriangular" | custom-call | tf_op jit(solution)/shard_map/jit(_solve_triangular)/triangular_solve | solution.py:63
  215.0 39.3 %custom-call.7 = f32[4,128,128]{1,2,0:T(8,128)S(1)} custom-call(f32[4,128,128]{2,1,0:T(8,128)S(1)} %get-tuple-element.28), custom_call_target="InvertDiagBlocksLowerTriangular" | custom-call | tf_op jit(solution)/shard_map/jit(_solve_triangular)/triangular_solve | solution.py:63
  254.4 2.6 fusion.23
  259.6 0.7 fusion.31
  260.6 21.2 %fusion.6 = f32[128,7680]{1,0:T(8,128)} fusion(f32[128,512]{1,0:T(8,128)S(1)} %copy-done.1, f32[8192,1536]{1,0:T(8,128)} %param.11, f32[128,8192]{1,0:T(8,128)} %copy-done), kind=kOutput, calls=%fused_computation.12 | convolution fusion | flops 6040780800 | bytes 23855104 | tf_op jit(solution)/shard_map/dot_general | solution.py:16
  281.8 49.3 %all-reduce.6.cloned.1.call-done = f32[128,512]{1,0:T(8,128)} async-done(((f32[128,512]{1,0:T(8,128)}), f32[128,512]{1,0:T(8,128)}) %all-reduce.6.cloned.1.call-update) | async-done | bytes 262160 | tf_op jit(solution)/shard_map/psum | solution.py:12
  331.0 2.6 fusion.22
  336.2 0.7 fusion.32
  336.9 23.0 %fusion.9 = f32[128,7680]{1,0:T(8,128)} fusion(f32[128,7680]{1,0:T(8,128)} %fusion.6, f32[128,512]{1,0:T(8,128)S(1)} %copy-done.2, f32[8192,1536]{1,0:T(8,128)} %param.11), kind=kOutput, calls=%fused_computation.13 | convolution fusion | flops 6040780800 | bytes 23855104 | tf_op jit(solution)/shard_map/dot_general | solution.py:16
  359.9 47.4 %all-reduce.8.cloned.1.call-done = f32[128,512]{1,0:T(8,128)} async-done(((f32[128,512]{1,0:T(8,128)}), f32[128,512]{1,0:T(8,128)}) %all-reduce.8.cloned.1.call-update) | async-done | bytes 262160 | tf_op jit(solution)/shard_map/psum | solution.py:12
  407.3 2.5 fusion.21
  409.8 20.4 %fusion.12 = f32[128,7680]{1,0:T(8,128)S(1)} fusion(f32[128,7680]{1,0:T(8,128)} %fusion.9, f32[128,512]{1,0:T(8,128)} %all-reduce.8.cloned.1.call-done, f32[8192,1536]{1,0:T(8,128)} %param.11), kind=kOutput, calls=%fused_computation.14 | convolution fusion | flops 6040780800 | bytes 23855104 | tf_op jit(solution)/shard_map/dot_general | solution.py:16
  430.2 2.3 pad_maximum_fusion
  (104 shorter events, 34.8 us)
Async XLA Ops:
  48.4 101.2 %all-to-all-start = ((f32[32,1,4,8192]{3,2,1,0:T(4,128)}), f32[32,1,4,8192]{3,2,1,0:T(4,128)}, u32[]{:S(2)}, u32[]{:S(2)}) async-start(f32[32,1,4,8192]{3,2,1,0:T(4,128)} %fusion.54), calls=%async_computation | async-start | bytes 8388608 | tf_op jit(solution)/shard_map/all_to_all | solution.py:44
  55.8 198.5 %all-reduce.4.cloned.1.call-start = ((), (), s32[]{:S(2)}) async-start(), calls=%async_computation.1 | async-start | bytes 524288 | tf_op jit(solution)/shard_map/psum | solution.py:12
  67.0 0.7 copy-start.4
  107.8 54.2 %copy-start.3 = (f32[4,128,128]{1,2,0:T(8,128)}, f32[4,128,128]{1,2,0:T(8,128)S(1)}, u32[]{:S(2)}) copy-start(f32[4,128,128]{1,2,0:T(8,128)S(1)} %custom-call.5) | copy-start | bytes 786436
  118.3 36.5 %copy-start.5 = (s32[1,128]{1,0:T(1,128)S(1)}, s32[1,128]{1,0:T(1,128)}, u32[]{:S(2)}) copy-start(s32[1,128]{1,0:T(1,128)} %param.10) | copy-start | bytes 1540
  159.3 2.0 copy-start
  166.4 164.6 %all-reduce.6.cloned.1.call-start = ((), (), s32[]{:S(2)}) async-start(), calls=%async_computation.2 | async-start | bytes 524288 | tf_op jit(solution)/shard_map/psum | solution.py:12
  254.4 6.2 %copy-start.1 = (f32[128,512]{1,0:T(8,128)S(1)}, f32[128,512]{1,0:T(8,128)}, u32[]{:S(2)}) copy-start(f32[128,512]{1,0:T(8,128)} %all-reduce.4.cloned.1.call-done) | copy-start | bytes 786436
  260.3 147.0 %all-reduce.8.cloned.1.call-start = ((), (), s32[]{:S(2)}) async-start(), calls=%async_computation.3 | async-start | bytes 524288 | tf_op jit(solution)/shard_map/psum | solution.py:12
  331.0 5.9 %copy-start.2 = (f32[128,512]{1,0:T(8,128)S(1)}, f32[128,512]{1,0:T(8,128)}, u32[]{:S(2)}) copy-start(f32[128,512]{1,0:T(8,128)} %all-reduce.6.cloned.1.call-done) | copy-start | bytes 786436
Sparse Core Ops, SparseCore 0:
  166.5 71.4 all-reduce.3
  260.5 70.5 all-reduce.5
  337.0 70.2 all-reduce.7
